TPU v7x, 32 devices: a whole 2x2x4 slice. The times are simulated.
32 devices in a mesh: groups: 2 (over x), port: 16 (over z, y, core).
Axes of the slice: x: 2, y: 2, z: 4, core: 2. Of those that a mesh axis runs over, the one named last changes fastest.
Arguments:
- measured: bfloat16 [4, 2, 4096, 4096], P('groups', None, 'port'), parts along dimension 0, may hold values from -6 to 6
- out_factor: bfloat16 [4096, 1024], P('port', 'groups'), parts along dimension 1, may hold values from -0.25 to 0.25
- in_factor: bfloat16 [1024, 4096], P('groups', 'port'), parts along dimension 0, may hold values from -6 to 6
- pole_rates: float32 [1024], P('groups'), parts along dimension 0, may hold values from 0.1 to 10
- freq_index: int32 [4], P('groups'), parts along dimension 0, may hold values from 0 to 1023
- quad_codes: int32 [4], P('groups'), parts along dimension 0, may hold values from 1 to 4
Outputs:
- grad_out: float32 [4096, 1024], P('port', 'groups'), parts along dimension 1
- grad_in_t: float32 [4096, 1024], P('port', 'groups'), parts along dimension 1
There are 2 independent parts, one for each index of `groups`. A program takes and returns all parts, laid end to end along the dimension named above; each array names one. Nothing has to cross between parts.
All inputs are finite; a program needn't handle non-finite values.
Results may differ from a plain program's by a relative error of at most 0.002.
Values may be sent and summed in bfloat16 or wider, within the bound.
A program may use at most 64 MiB of HBM per device.

v0:
```python
import math

import jax
import jax.numpy as jnp
from jax import lax
from jax.sharding import PartitionSpec as P

GRID = 1024


low_freq = 0.1
log_span = math.log(100.0)


def pole_terms(freq_index, pole_rates):
    omega = low_freq * jnp.exp(log_span * freq_index.astype(jnp.float32) / (GRID - 1))
    denominator = pole_rates[None, :] * pole_rates[None, :] + omega[:, None] * omega[:, None]
    real_side = pole_rates[None, :] / denominator
    imag_side = -omega[:, None] / denominator
    return jnp.stack([real_side, imag_side], axis=1)


def contract_first(left, right):
    return lax.dot_general(
        left, right, (((0,), (0,)), ((), ())), preferred_element_type=jnp.float32
    )


def contract_second(left, right):
    return lax.dot_general(
        left, right, (((1,), (1,)), ((), ())), preferred_element_type=jnp.float32
    )


def on_device(measured, out_factor, in_factor, pole_rates, freq_index, quad_codes):
    freq_count = measured.shape[0]
    local_rows = out_factor.shape[0]
    pole_count = out_factor.shape[1]
    local_cols = in_factor.shape[1]
    total_in = measured.shape[3]
    total_out = local_rows * lax.axis_size("port")
    coefficients = pole_terms(freq_index, pole_rates)
    weights = quad_codes.astype(jnp.float32) * 0.25
    weighted = weights[:, None, None] * coefficients
    scaled = (
        out_factor.astype(jnp.float32)[None, None, :, :] * coefficients[:, :, None, :]
    ).astype(jnp.bfloat16)
    block_cols = lax.all_gather(in_factor, "port", axis=1, tiled=True)
    width_cols = block_cols.shape[1]
    model = jnp.dot(scaled.reshape(-1, pole_count), block_cols, preferred_element_type=jnp.float32)
    model = model.reshape(freq_count, 2, local_rows, width_cols)
    residual = (model - measured.astype(jnp.float32)).astype(jnp.bfloat16)
    update = contract_second(residual.reshape(-1, width_cols), block_cols)
    update = update.reshape(freq_count, 2, local_rows, pole_count)
    grad_out = jnp.zeros((local_rows, pole_count), jnp.float32)
    for freq_slot in range(freq_count):
        for comp_slot in range(2):
            grad_out = (
                grad_out + weighted[freq_slot, comp_slot][None, :] * update[freq_slot, comp_slot]
            )
    grad_out = grad_out * (1.0 / math.sqrt(total_in))
    running = jnp.zeros((local_cols * lax.axis_size("port"), pole_count), jnp.float32)
    for freq_slot in range(freq_count):
        for comp_slot in range(2):
            running = running + weighted[freq_slot, comp_slot][None, :] * contract_first(
                residual[freq_slot, comp_slot], out_factor
            )
    grad_in_t = lax.psum_scatter(running, "port", scatter_dimension=0, tiled=True)
    grad_in_t = grad_in_t * (1.0 / math.sqrt(total_out))
    return (grad_out, grad_in_t)


def solution(mesh):
    in_specs = (
        P("groups", None, "port", None),
        P("port", "groups"),
        P("groups", "port"),
        P("groups"),
        P("groups"),
        P("groups"),
    )
    out_specs = (P("port", "groups"), P("port", "groups"))
    return jax.shard_map(
        on_device, mesh=mesh, in_specs=in_specs, out_specs=out_specs, check_vma=False
    )
```

profile of v0, /device:TPU:0, one launch (start us, length us, event | category | flops | bytes accessed | tf_op | source)
XLA Modules:
  0.0 206.1 jit_solution(8669891354242152455)
XLA Ops:
  7.2 0.0 all-gather.2.cloned.1.call-start
  7.2 0.7 all-gather.2.cloned.1.call-update
  7.9 0.0 reduce-scatter.2.cloned.1.call-start
  7.9 0.8 mul.118
  8.7 1.0 convert_element_type.22
  9.7 0.7 convert_multiply_fusion
  10.4 0.7 fusion.17
  11.0 0.8 add_divide_fusion.1
  11.8 0.1 broadcast_multiply_fusion.1
  11.9 53.5 %all-gather.2.cloned.1.call-done = bf16[512,4096]{1,0:T(8,128)(2,1)} async-done(((bf16[512,256]{1,0:T(8,128)(2,1)}), bf16[512,4096]{1,0:T(8,128)(2,1)}) %all-gather.2.cloned.1.call-update) | async-done | bytes 4194320 | tf_op jit(solution)/shard_map/all_gather | solution.py:48
  65.4 0.0 copy-start.1
  65.4 8.3 %subtract_convert_fusion = bf16[2,2,256,4096]{3,2,1,0:T(8,128)(2,1)S(1)} fusion(bf16[2,2,256,4096]{3,2,1,0:T(8,128)(2,1)} %param.6, bf16[512,4096]{1,0:T(8,128)(2,1)} %all-gather.2.cloned.1.call-done, f32[2,2,512]{2,1,0:T(2,128)S(1)} %get-tuple-element.7, f32[256,512]{1,0:T(8,128)S(1)} %convert_element_type.22), kind=kOutput, calls=%fused_computation | convolution fusion | flops 4308598784 | bytes 21504000 | tf_op jit(solution)/shard_map/dot_general | solution.py:50
  73.6 0.0 copy-start
  73.7 3.2 %copy-done = bf16[2,2,256,4096]{3,2,1,0:T(8,128)(2,1)} copy-done((bf16[2,2,256,4096]{3,2,1,0:T(8,128)(2,1)}, bf16[2,2,256,4096]{3,2,1,0:T(8,128)(2,1)S(1)}, u32[]{:S(2)}) %copy-start) | copy-done | bytes 8388632
  76.9 0.0 copy-done.1
  76.9 1.3 fusion.3
  78.2 2.9 %fusion.4 = f32[4096,512]{1,0:T(8,128)S(1)} fusion(bf16[256,512]{1,0:T(8,128)(2,1)S(1)} %copy-done.1, bf16[2,2,256,4096]{3,2,1,0:T(8,128)(2,1)} %copy-done), kind=kOutput, calls=%fused_computation.9 | convolution fusion | flops 1073741824 | bytes 10747904 | tf_op jit(solution)/shard_map/dot_general | solution.py:24
  81.1 6.1 %fusion.5 = f32[4096,512]{1,0:T(8,128)} fusion(bf16[256,512]{1,0:T(8,128)(2,1)S(1)} %copy-done.1, bf16[2,2,256,4096]{3,2,1,0:T(8,128)(2,1)} %copy-done), kind=kOutput, calls=%fused_computation.11 | convolution fusion | flops 1073741824 | bytes 10747904 | tf_op jit(solution)/shard_map/dot_general | solution.py:24
  87.2 8.4 %multiply_add_fusion = f32[4096,512]{1,0:T(8,128)} fusion(f32[4096,512]{1,0:T(8,128)S(1)} %fusion.3, f32[4096,512]{1,0:T(8,128)S(1)} %fusion.4, f32[4096,512]{1,0:T(8,128)} %fusion.5, bf16[256,512]{1,0:T(8,128)(2,1)S(1)} %copy-done.1, f32[512]{0:T(512)S(1)} %bitcast.60, f32[512]{0:T(512)S(1)} %bitcast.62, f32[512]{0:T(512)S(1)} %bitcast.64, ...), kind=kOutput, calls=%fused_computation.1 | convolution fusion | flops 1088421888 | bytes 35921920 | tf_op jit(solution)/shard_map/dot_general | solution.py:24
  95.6 0.0 reduce-scatter.2.cloned.1.call-update
  95.6 8.2 %fusion = f32[2,2,256,512]{3,2,1,0:T(8,128)S(1)} fusion(bf16[2,2,256,4096]{3,2,1,0:T(8,128)(2,1)} %copy-done, bf16[512,4096]{1,0:T(8,128)(2,1)} %all-gather.2.cloned.1.call-done), kind=kOutput, calls=%fused_computation.2 | convolution fusion | flops 4294967296 | bytes 14680064 | tf_op jit(solution)/shard_map/dot_general | solution.py:30
  103.9 1.0 fusion.10
  104.9 92.5 %reduce-scatter.2.cloned.1.call-done = f32[256,512]{1,0:T(8,128)} async-done(((f32[4096,512]{1,0:T(8,128)}), f32[256,512]{1,0:T(8,128)}) %reduce-scatter.2.cloned.1.call-update) | async-done | bytes 524304 | tf_op jit(solution)/shard_map/reduce_scatter | solution.py:68
  197.4 1.9 broadcast_multiply_fusion
  (1 shorter events, 0.0 us)
Async XLA Ops:
  7.2 58.2 %all-gather.2.cloned.1.call-start = ((), (), s32[]{:S(2)}) async-start(), calls=%async_computation.1 | async-start | bytes 4456448 | tf_op jit(solution)/shard_map/all_gather | solution.py:48
  7.9 189.5 %reduce-scatter.2.cloned.1.call-start = ((), (), s32[]{:S(2)}) async-start(), calls=%async_computation.2 | async-start | bytes 8912896 | tf_op jit(solution)/shard_map/reduce_scatter | solution.py:68
  65.4 11.5 %copy-start.1 = (bf16[256,512]{1,0:T(8,128)(2,1)S(1)}, bf16[256,512]{1,0:T(8,128)(2,1)}, u32[]{:S(2)}) copy-start(bf16[256,512]{1,0:T(8,128)(2,1)} %param.7) | copy-start | bytes 786436
  73.6 3.2 %copy-start = (bf16[2,2,256,4096]{3,2,1,0:T(8,128)(2,1)}, bf16[2,2,256,4096]{3,2,1,0:T(8,128)(2,1)S(1)}, u32[]{:S(2)}) copy-start(bf16[2,2,256,4096]{3,2,1,0:T(8,128)(2,1)S(1)} %subtract_convert_fusion) | copy-start | bytes 25165828
Sparse Core Ops, SparseCore 0:
  10.1 55.1 all-gather.1
  95.8 101.5 reduce-scatter.1
where the time goes:
time: 206 us
  waiting for transfers between devices  147 us (71%)
  matrix products  35.2 us (17%)
  between operations  14.1 us (7%)
  other arithmetic  6.84 us (3%)
  local copies, waits for them, and re-layouts  3.23 us (2%)
    reduce_scatter x1, waiting for transfers between devices, on_device(): lax.psum_scatter(running, 'port', scatter_dimension=0, tiled=True)  92.5 us
    all_gather x1, waiting for transfers between devices, on_device(): block_cols = lax.all_gather(in_factor, 'port', axis=1, tiled=True)  53.5 us
    dot_general x4, matrix products, contract_first(): lax.dot_general(left, right, (((0,), (0,)), ((), ())), preferred_element_...  18.7 us
    dot_general x1, matrix products, on_device(): jnp.dot(scaled.reshape(-1, pole_count), block_cols, preferred_element_typ...  8.27 us
    dot_general x1, matrix products, contract_second(): lax.dot_general(left, right, (((1,), (1,)), ((), ())), preferred_element_...  8.24 us
  transfers between devices with their start and end apart: 2, of which 2 were waited for; matrix products, arithmetic and copies ran while one was open for 6% of the time, Pallas kernels for 0%

commit v1 on v0

v1 whole, which is shorter than its diff:
```python
import functools
import math

import jax
import jax.numpy as jnp
from jax import lax
from jax.experimental import pallas as pl
from jax.experimental.pallas import tpu as pltpu
from jax.sharding import PartitionSpec as P

GRID = 1024
MESH = pl.DeviceIdType.MESH
RS_TYPE = jnp.float32

low_freq = 0.1
log_span = math.log(100.0)


def contract_second(left, right):
    return lax.dot_general(
        left, right, (((1,), (1,)), ((), ())), preferred_element_type=jnp.float32
    )


def contract_first(left, right):
    return lax.dot_general(
        left, right, (((0,), (0,)), ((), ())), preferred_element_type=jnp.float32
    )


def pole_terms(freq_index, pole_rates):
    omega = low_freq * jnp.exp(log_span * freq_index.astype(jnp.float32) / (GRID - 1))
    denominator = pole_rates[None, :] * pole_rates[None, :] + omega[:, None] * omega[:, None]
    real_side = pole_rates[None, :] / denominator
    imag_side = -omega[:, None] / denominator
    return jnp.stack([real_side, imag_side], axis=1)


def kernel(
    chips, total_out, total_in,
    measured, out_factor, in_factor, rates, freq, quad,
    grad_out, grad_in,
    own, sib_b, meas, scaled, out_t, w_row, w_col, acc, g_own, g_send, g_recv, rs_send, rs_recv,
    loc_sem, meas_sem, ag_s, ag_r, sb_s, sb_r, gs_s, gs_r, rs_s, rs_r,
):
    combos = scaled.shape[0]
    rows, poles = out_factor.shape
    cols = in_factor.shape[1]
    half = chips // 2

    def chip_at(place):
        upper = place // half
        return (1 - upper) * (2 * place) + upper * (2 * (chips - 1 - place) + 1)

    me = lax.axis_index("port")
    core = me % 2
    chip = me // 2
    row_y = chip % 2
    col_z = chip // 2
    place = (1 - row_y) * col_z + row_y * (chips - 1 - col_z)
    sign = 1 - 2 * core
    nxt = chip_at((place + sign + chips) % chips) * 2 + core
    prv = chip_at((place - sign + chips) % chips) * 2 + core
    sib = chip * 2 + 1 - core

    local = pltpu.make_async_copy(in_factor, own.at[0], loc_sem)
    local.start()

    def meas_copy(which, step):
        if which == 0:
            block = chip_at((place - step * sign + chips) % chips) * 2 + core
        else:
            block = chip_at((place + step * sign + chips) % chips) * 2 + 1 - core
        first = pl.multiple_of(block * cols, cols)
        return pltpu.make_async_copy(
            measured.at[:, :, pl.ds(first, cols)], meas.at[which, step], meas_sem.at[which, step]
        )

    barrier = pltpu.get_barrier_semaphore()
    for other in (nxt, prv, sib):
        pl.semaphore_signal(barrier, inc=1, device_id={"port": other}, device_id_type=MESH)

    def remote(src, dst, send, recv, target):
        return pltpu.make_async_remote_copy(
            src_ref=src, dst_ref=dst, send_sem=send, recv_sem=recv,
            device_id={"port": target}, device_id_type=MESH,
        )

    def ag_copy(step):
        return remote(own.at[step], own.at[step + 1], ag_s.at[step], ag_r.at[step + 1], nxt)

    def ag_arrival(step):
        return remote(own.at[step], own.at[step], ag_s.at[step], ag_r.at[step], nxt)

    def sb_copy(step):
        return remote(own.at[step], sib_b.at[step], sb_s.at[step], sb_r.at[step], sib)

    def gs_copy(step):
        return remote(g_send.at[step], g_recv.at[step], gs_s.at[step], gs_r.at[step], sib)

    def rs_copy(step):
        return remote(rs_send.at[step], rs_recv.at[step + 1], rs_s.at[step], rs_r.at[step + 1], nxt)

    def rs_arrival(step):
        return remote(rs_recv.at[step], rs_recv.at[step], rs_s.at[step], rs_r.at[step], nxt)

    pl.semaphore_wait(barrier, 3)
    local.wait()
    ag_copy(0).start()
    sb_copy(0).start()

    @pl.loop(0, chips)
    def _(step):
        meas_copy(0, step).start()
        meas_copy(1, step).start()

    rate = rates[...]
    factor = out_factor[...].astype(jnp.float32)
    out_t[...] = factor.T.astype(jnp.bfloat16)
    for slot in range(combos // 2):
        omega = low_freq * jnp.exp(
            log_span * freq[slot : slot + 1, :].astype(jnp.float32) / (GRID - 1)
        )
        weight = quad[slot : slot + 1, :].astype(jnp.float32) * 0.25
        denominator = rate * rate + omega * omega
        for part, coef in enumerate((rate / denominator, -omega / denominator)):
            k = 2 * slot + part
            scaled[k] = (factor * coef).astype(jnp.bfloat16)
            w_row[k] = jnp.broadcast_to(weight * coef, (8, poles))
            w_col[k] = jnp.broadcast_to(weight * coef, (128, poles)).T
            acc[k] = jnp.zeros((rows, poles), jnp.float32)

    def handle_gather(step):
        ag_arrival(step).wait_recv()

        @pl.when(step < chips - 1)
        def _():
            ag_copy(step).start()

        sb_copy(step).start()

    def compute(step):
        sb_copy(step).wait_recv()
        meas_copy(0, step).wait()
        meas_copy(1, step).wait()
        left = own[step]
        right = sib_b[step]
        gin_own = None
        gin_sib = None
        for k in range(combos):
            stretched = jnp.concatenate([w_col[k]] * (cols // 128), axis=1)
            lhs = scaled[k]
            model = jnp.dot(lhs, left, preferred_element_type=jnp.float32)
            res_own = (model - meas[0, step, k].astype(jnp.float32)).astype(jnp.bfloat16)
            model = jnp.dot(lhs, right, preferred_element_type=jnp.float32)
            res_sib = (model - meas[1, step, k].astype(jnp.float32)).astype(jnp.bfloat16)
            acc[k] += contract_second(res_own, left) + contract_second(res_sib, right)
            transposed = out_t[...]
            part = stretched * jnp.dot(transposed, res_own, preferred_element_type=jnp.float32)
            gin_own = part if gin_own is None else gin_own + part
            part = stretched * jnp.dot(transposed, res_sib, preferred_element_type=jnp.float32)
            gin_sib = part if gin_sib is None else gin_sib + part
        g_send[step] = gin_sib
        gs_copy(step).start()
        g_own[step] = gin_own

    def handle_sum(step):
        gs_copy(step).wait_recv()

        @pl.when(step == 1)
        def _():
            rs_send[step] = (g_own[step] + g_recv[step]).astype(RS_TYPE)

        @pl.when(step > 1)
        def _():
            rs_arrival(step).wait_recv()
            rs_send[step] = (
                g_own[step] + g_recv[step] + rs_recv[step].astype(jnp.float32)
            ).astype(RS_TYPE)

        @pl.when(step > 0)
        def _():
            rs_copy(step).start()

    @pl.loop(0, chips)
    def _(step):
        @pl.when((step > 0) & (step < chips - 1))
        def _():
            handle_gather(step + 1)

        compute(step)

        @pl.when(step == 0)
        def _():
            handle_gather(step + 1)

        @pl.when(step > 0)
        def _():
            handle_sum(step - 1)

    handle_sum(chips - 1)

    total = jnp.zeros((rows, poles), jnp.float32)
    for k in range(combos):
        total = total + w_row[k][0:1, :] * acc[k]
    grad_out[...] = total * (1.0 / math.sqrt(total_in))

    rs_arrival(chips).wait_recv()
    summed = g_own[0] + g_recv[0] + rs_recv[chips].astype(jnp.float32)
    grad_in[...] = (summed * (1.0 / math.sqrt(total_out))).T

    @pl.loop(0, chips)
    def _(step):
        sb_copy(step).wait_send()
        gs_copy(step).wait_send()

        @pl.when(step < chips - 1)
        def _():
            ag_copy(step).wait_send()

        @pl.when(step > 0)
        def _():
            rs_copy(step).wait_send()


def fused(measured, out_factor, in_factor, pole_rates, freq_index, quad_codes):
    combos = measured.shape[0] * 2
    rows, poles = out_factor.shape
    cols = in_factor.shape[1]
    total_in = measured.shape[3]
    ports = lax.axis_size("port")
    total_out = rows * ports
    chips = ports // 2
    vmem = pl.BlockSpec(memory_space=pltpu.VMEM)
    anywhere = pl.BlockSpec(memory_space=pl.ANY)
    dma = pltpu.SemaphoreType.DMA
    call = pl.pallas_call(
        functools.partial(kernel, chips, total_out, total_in),
        out_shape=(
            jax.ShapeDtypeStruct((rows, poles), jnp.float32),
            jax.ShapeDtypeStruct((cols, poles), jnp.float32),
        ),
        in_specs=[anywhere, vmem, anywhere, vmem, vmem, vmem],
        out_specs=(vmem, vmem),
        scratch_shapes=[
            pltpu.VMEM((chips, poles, cols), jnp.bfloat16),
            pltpu.VMEM((chips, poles, cols), jnp.bfloat16),
            pltpu.VMEM((2, chips, combos, rows, cols), jnp.bfloat16),
            pltpu.VMEM((combos, rows, poles), jnp.bfloat16),
            pltpu.VMEM((poles, rows), jnp.bfloat16),
            pltpu.VMEM((combos, 8, poles), jnp.float32),
            pltpu.VMEM((combos, poles, 128), jnp.float32),
            pltpu.VMEM((combos, rows, poles), jnp.float32),
            pltpu.VMEM((chips, poles, cols), jnp.float32),
            pltpu.VMEM((chips, poles, cols), jnp.float32),
            pltpu.VMEM((chips, poles, cols), jnp.float32),
            pltpu.VMEM((chips, poles, cols), RS_TYPE),
            pltpu.VMEM((chips + 1, poles, cols), RS_TYPE),
            dma,
            dma((2, chips)),
            dma((chips,)),
            dma((chips + 1,)),
            dma((chips,)),
            dma((chips,)),
            dma((chips,)),
            dma((chips,)),
            dma((chips + 1,)),
            dma((chips + 1,)),
        ],
        compiler_params=pltpu.CompilerParams(
            collective_id=0, has_side_effects=True, vmem_limit_bytes=60 * 1024 * 1024
        ),
    )
    return call(
        measured.reshape(combos, rows, total_in),
        out_factor,
        in_factor,
        pole_rates.reshape(1, poles),
        freq_index.reshape(-1, 1),
        quad_codes.reshape(-1, 1),
    )


def plain(measured, out_factor, in_factor, pole_rates, freq_index, quad_codes):
    freq_count = measured.shape[0]
    local_rows, pole_count = out_factor.shape
    local_cols = in_factor.shape[1]
    total_in = measured.shape[3]
    total_out = local_rows * lax.axis_size("port")
    coefficients = pole_terms(freq_index, pole_rates)
    weights = quad_codes.astype(jnp.float32) * 0.25
    weighted = weights[:, None, None] * coefficients
    scaled = (
        out_factor.astype(jnp.float32)[None, None, :, :] * coefficients[:, :, None, :]
    ).astype(jnp.bfloat16)
    block_cols = lax.all_gather(in_factor, "port", axis=1, tiled=True)
    width_cols = block_cols.shape[1]
    model = jnp.dot(scaled.reshape(-1, pole_count), block_cols, preferred_element_type=jnp.float32)
    model = model.reshape(freq_count, 2, local_rows, width_cols)
    residual = (model - measured.astype(jnp.float32)).astype(jnp.bfloat16)
    update = contract_second(residual.reshape(-1, width_cols), block_cols)
    update = update.reshape(freq_count, 2, local_rows, pole_count)
    grad_out = jnp.sum(weighted[:, :, None, :] * update, axis=(0, 1))
    grad_out = grad_out * (1.0 / math.sqrt(total_in))
    running = jnp.zeros((width_cols, pole_count), jnp.float32)
    for freq_slot in range(freq_count):
        for comp_slot in range(2):
            running = running + weighted[freq_slot, comp_slot][None, :] * contract_first(
                residual[freq_slot, comp_slot], out_factor
            )
    grad_in_t = lax.psum_scatter(running, "port", scatter_dimension=0, tiled=True)
    return (grad_out, grad_in_t * (1.0 / math.sqrt(total_out)))


def on_device(measured, out_factor, in_factor, pole_rates, freq_index, quad_codes):
    whole_lanes = in_factor.shape[1] % 128 == 0 and out_factor.shape[1] % 128 == 0
    body = fused if whole_lanes and lax.axis_size("port") % 8 == 0 else plain
    return body(measured, out_factor, in_factor, pole_rates, freq_index, quad_codes)


def solution(mesh):
    in_specs = (
        P("groups", None, "port", None),
        P("port", "groups"),
        P("groups", "port"),
        P("groups"),
        P("groups"),
        P("groups"),
    )
    out_specs = (P("port", "groups"), P("port", "groups"))
    return jax.shard_map(
        on_device, mesh=mesh, in_specs=in_specs, out_specs=out_specs, check_vma=False
    )
```

time: 206 us -> 90.9 us (0.44)
  waiting for transfers between devices: 147 us -> 0 us
  Pallas kernels: 0 us -> 83.7 us
  matrix products: 35.2 us -> 0 us
  between operations: 14.1 us -> 0.64 us
  other arithmetic: 6.84 us -> 0 us
  local copies, waits for them, and re-layouts: 3.23 us -> 6.33 us
    reduce_scatter x1 -> x0, waiting for transfers between devices: 92.5 us -> none  [on_device(): lax.psum_scatter(running, 'port', scatter_dimension=0, tiled=True)]
    pallas_call x0 -> x1, Pallas kernels: none -> 83.7 us  [fused(): call(measured.reshape(combos, rows, total_in), out_factor, in_factor, pol...]
    all_gather x1 -> x0, waiting for transfers between devices: 53.5 us -> none  [on_device(): block_cols = lax.all_gather(in_factor, 'port', axis=1, tiled=True)]
    dot_general x6 -> x0, matrix products: 35.2 us -> none  [the longest x4 18.7 us: contract_first(): lax.dot_general(left, right, (((0,), (0,)), ((), ())), preferred_element_...]
    mul x6 -> x0, other arithmetic: 5.08 us -> none  [the longest x1 1.87 us: on_device(): grad_in_t = grad_in_t * (1.0 / math.sqrt(total_out))]
    reshape x0 -> x2, local copies, waits for them, and re-layouts: none -> 2.59 us  [the longest x1 1.3 us: fused(): freq_index.reshape(-1, 1)]
  transfers between devices with their start and end apart: 2 -> 0, of which waited for: 2 -> 0; matrix products, arithmetic and copies ran while one was open for 6% -> 0% of each run, Pallas kernels for 0% -> 0%
where the time goes in v1:
time: 90.9 us; the launch traced here: 90.6 us
  Pallas kernels  83.7 us (92%)
  local copies, waits for them, and re-layouts  6.33 us (7%)
    pallas_call x1, Pallas kernels, fused(): call(measured.reshape(combos, rows, total_in), out_factor, in_factor, pol...  83.7 us
    unnamed x2, local copies, waits for them, and re-layouts  3.74 us

profile of v1, /device:TPU:0, one launch (start us, length us, event | category | flops | bytes accessed | tf_op | source)
XLA Modules:
  0.0 90.6 jit_solution(6927412157907182403)
XLA Ops:
  0.6 1.3 %copy.8.freq = s32[2,1]{1,0:T(2,128)} copy(s32[2,1]{0,1:T(1,128)} %bitcast.6) | data formatting | bytes 16 | tf_op jit(solution)/shard_map/reshape | solution.py:279
  1.9 1.3 %copy.9.quad = s32[2,1]{1,0:T(2,128)} copy(s32[2,1]{0,1:T(1,128)} %bitcast.7) | data formatting | bytes 16 | tf_op jit(solution)/shard_map/reshape | solution.py:280
  3.2 83.7 %shard_map.77 = (f32[256,512]{1,0:T(8,128)}, f32[256,512]{1,0:T(8,128)}) custom-call(bf16[4,256,4096]{2,1,0:T(8,128)(2,1)} %bitcast.4, bf16[256,512]{1,0:T(8,128)(2,1)} %out_factor.1, bf16[512,256]{1,0:T(8,128)(2,1)} %in_factor.1, f32[1,512]{1,0:T(1,128)} %bitcast.5, s32[2,1]{1,0:T(2,128)} %copy.8.freq, s32[2,1]{1,0:T(2,128)} %copy.9.quad), custom_call_target="tpu_custom_call" | custom-call | tf_op jit(solution)/shard_map/pallas_call | solution.py:274
  86.9 1.9 %copy.12 = f32[256,512]{1,0:T(8,128)} copy(f32[256,512]{1,0:T(8,128)} %get-tuple-element.4) | data formatting | bytes 1048576
  88.8 1.9 %copy.13 = f32[256,512]{1,0:T(8,128)} copy(f32[256,512]{1,0:T(8,128)} %get-tuple-element.5) | data formatting | bytes 1048576

commit v2 on v1

--- a/solution.py
+++ b/solution.py
@@ -10,7 +10,7 @@
 
 GRID = 1024
 MESH = pl.DeviceIdType.MESH
-RS_TYPE = jnp.float32
+CODE = 16
 
 low_freq = 0.1
 log_span = math.log(100.0)
@@ -37,7 +37,7 @@
 
 
 def kernel(
-    chips, total_out, total_in,
+    chips,
     measured, out_factor, in_factor, rates, freq, quad,
     grad_out, grad_in,
     own, sib_b, meas, scaled, out_t, w_row, w_col, acc, g_own, g_send, g_recv, rs_send, rs_recv,
@@ -118,10 +118,9 @@
     factor = out_factor[...].astype(jnp.float32)
     out_t[...] = factor.T.astype(jnp.bfloat16)
     for slot in range(combos // 2):
-        omega = low_freq * jnp.exp(
-            log_span * freq[slot : slot + 1, :].astype(jnp.float32) / (GRID - 1)
-        )
-        weight = quad[slot : slot + 1, :].astype(jnp.float32) * 0.25
+        position = jnp.full((1, poles), freq[slot], jnp.int32).astype(jnp.float32)
+        omega = low_freq * jnp.exp(log_span * position / (GRID - 1))
+        weight = jnp.full((1, poles), quad[slot], jnp.int32).astype(jnp.float32) * 0.25
         denominator = rate * rate + omega * omega
         for part, coef in enumerate((rate / denominator, -omega / denominator)):
             k = 2 * slot + part
@@ -164,19 +163,29 @@
         gs_copy(step).start()
         g_own[step] = gin_own
 
+    def encode(step, value):
+        largest = jnp.maximum(jnp.max(jnp.abs(value), axis=0, keepdims=True), 1e-30)
+        exponent = jnp.ceil(jnp.log2(largest) + 0.01) - 15.0
+        coded = jnp.round(value * jnp.exp2(-exponent))
+        rs_send[step, :poles, :] = coded.astype(jnp.int32).astype(jnp.int16)
+        tail = jnp.broadcast_to(exponent.astype(jnp.int32), (CODE, cols))
+        rs_send[step, poles:, :] = tail.astype(jnp.int16)
+
+    def decode(step):
+        tail = rs_recv[step, poles:, :].astype(jnp.int32).astype(jnp.float32)
+        return rs_recv[step, :poles, :].astype(jnp.int32).astype(jnp.float32) * jnp.exp2(tail[0:1])
+
     def handle_sum(step):
         gs_copy(step).wait_recv()
 
         @pl.when(step == 1)
         def _():
-            rs_send[step] = (g_own[step] + g_recv[step]).astype(RS_TYPE)
+            encode(step, g_own[step] + g_recv[step])
 
         @pl.when(step > 1)
         def _():
             rs_arrival(step).wait_recv()
-            rs_send[step] = (
-                g_own[step] + g_recv[step] + rs_recv[step].astype(jnp.float32)
-            ).astype(RS_TYPE)
+            encode(step, g_own[step] + g_recv[step] + decode(step))
 
         @pl.when(step > 0)
         def _():
@@ -203,11 +212,11 @@
     total = jnp.zeros((rows, poles), jnp.float32)
     for k in range(combos):
         total = total + w_row[k][0:1, :] * acc[k]
-    grad_out[...] = total * (1.0 / math.sqrt(total_in))
+    grad_out[...] = total
 
     rs_arrival(chips).wait_recv()
-    summed = g_own[0] + g_recv[0] + rs_recv[chips].astype(jnp.float32)
-    grad_in[...] = (summed * (1.0 / math.sqrt(total_out))).T
+    summed = g_own[0] + g_recv[0] + decode(chips)
+    grad_in[...] = summed.T
 
     @pl.loop(0, chips)
     def _(step):
@@ -233,14 +242,15 @@
     chips = ports // 2
     vmem = pl.BlockSpec(memory_space=pltpu.VMEM)
     anywhere = pl.BlockSpec(memory_space=pl.ANY)
+    scalar = pl.BlockSpec(memory_space=pltpu.SMEM)
     dma = pltpu.SemaphoreType.DMA
     call = pl.pallas_call(
-        functools.partial(kernel, chips, total_out, total_in),
+        functools.partial(kernel, chips),
         out_shape=(
             jax.ShapeDtypeStruct((rows, poles), jnp.float32),
             jax.ShapeDtypeStruct((cols, poles), jnp.float32),
         ),
-        in_specs=[anywhere, vmem, anywhere, vmem, vmem, vmem],
+        in_specs=[anywhere, vmem, anywhere, vmem, scalar, scalar],
         out_specs=(vmem, vmem),
         scratch_shapes=[
             pltpu.VMEM((chips, poles, cols), jnp.bfloat16),
@@ -254,8 +264,8 @@
             pltpu.VMEM((chips, poles, cols), jnp.float32),
             pltpu.VMEM((chips, poles, cols), jnp.float32),
             pltpu.VMEM((chips, poles, cols), jnp.float32),
-            pltpu.VMEM((chips, poles, cols), RS_TYPE),
-            pltpu.VMEM((chips + 1, poles, cols), RS_TYPE),
+            pltpu.VMEM((chips, poles + CODE, cols), jnp.int16),
+            pltpu.VMEM((chips + 1, poles + CODE, cols), jnp.int16),
             dma,
             dma((2, chips)),
             dma((chips,)),
@@ -271,14 +281,15 @@
             collective_id=0, has_side_effects=True, vmem_limit_bytes=60 * 1024 * 1024
         ),
     )
-    return call(
+    grad_out, grad_in = call(
         measured.reshape(combos, rows, total_in),
         out_factor,
         in_factor,
         pole_rates.reshape(1, poles),
-        freq_index.reshape(-1, 1),
-        quad_codes.reshape(-1, 1),
-    )
+        freq_index,
+        quad_codes,
+    )
+    return grad_out * (1.0 / math.sqrt(total_in)), grad_in * (1.0 / math.sqrt(total_out))
 
 
 def plain(measured, out_factor, in_factor, pole_rates, freq_index, quad_codes):

time: 90.9 us -> 68.4 us (0.75)
  Pallas kernels: 83.7 us -> 65.3 us
  local copies, waits for them, and re-layouts: 6.33 us -> 0 us
  other arithmetic: 0 us -> 2.26 us
    pallas_call x1, Pallas kernels: 83.7 us -> 65.3 us  [fused(): call(measured.reshape(combos, rows, total_in), out_factor, in_factor, pol...]
    unnamed x2 -> x0, local copies, waits for them, and re-layouts: 3.74 us -> none
    reshape x2 -> x0, local copies, waits for them, and re-layouts: 2.59 us -> none  [the longest x1 1.3 us: fused(): freq_index.reshape(-1, 1)]
    mul x0 -> x1, other arithmetic: none -> 2.26 us  [fused(): grad_in * (1.0 / math.sqrt(total_out))]
where the time goes in v2:
time: 68.4 us; the launch traced here: 68.2 us
  Pallas kernels  65.3 us (95%)
  other arithmetic  2.26 us (3%)
    pallas_call x1, Pallas kernels, fused(): call(measured.reshape(combos, rows, total_in), out_factor, in_factor, pol...  65.3 us
    mul x1, other arithmetic, fused(): grad_in * (1.0 / math.sqrt(total_out))  2.26 us

profile of v2, /device:TPU:0, one launch (start us, length us, event | category | flops | bytes accessed | tf_op | source)
XLA Modules:
  0.0 68.2 jit_solution(5135351967854157246)
XLA Ops:
  0.6 65.3 %shard_map.77 = (f32[256,512]{1,0:T(8,128)}, f32[256,512]{1,0:T(8,128)}) custom-call(bf16[4,256,4096]{2,1,0:T(8,128)(2,1)} %bitcast.2, bf16[256,512]{1,0:T(8,128)(2,1)} %out_factor.1, bf16[512,256]{1,0:T(8,128)(2,1)} %in_factor.1, f32[1,512]{1,0:T(1,128)} %bitcast.3, s32[2]{0:T(128)} %freq.1, s32[2]{0:T(128)} %quad.1), custom_call_target="tpu_custom_call" | custom-call | tf_op jit(solution)/shard_map/pallas_call | solution.py:284
  65.9 2.3 %broadcast_multiply_fusion = (f32[256,512]{1,0:T(8,128)}, f32[256,512]{1,0:T(8,128)}) fusion(f32[256,512]{1,0:T(8,128)} %get-tuple-element.5, f32[256,512]{1,0:T(8,128)} %get-tuple-element.4), kind=kLoop, calls=%fused_computation | loop fusion | flops 262144 | bytes 2097152 | tf_op jit(solution)/shard_map/mul | solution.py:292

commit v3 on v2

--- a/solution.py
+++ b/solution.py
@@ -11,6 +11,7 @@
 GRID = 1024
 MESH = pl.DeviceIdType.MESH
 CODE = 16
+PIECES = 2
 
 low_freq = 0.1
 log_span = math.log(100.0)
@@ -86,11 +87,17 @@
             device_id={"port": target}, device_id_type=MESH,
         )
 
-    def ag_copy(step):
-        return remote(own.at[step], own.at[step + 1], ag_s.at[step], ag_r.at[step + 1], nxt)
-
-    def ag_arrival(step):
-        return remote(own.at[step], own.at[step], ag_s.at[step], ag_r.at[step], nxt)
+    share = poles // PIECES
+
+    def ag_copy(step, piece, ahead=1):
+        part = pl.ds(piece * share, share)
+        return remote(
+            own.at[step, part], own.at[step + ahead, part],
+            ag_s.at[step, piece], ag_r.at[step + ahead, piece], nxt,
+        )
+
+    def ag_arrival(step, piece):
+        return ag_copy(step, piece, 0)
 
     def sb_copy(step):
         return remote(own.at[step], sib_b.at[step], sb_s.at[step], sb_r.at[step], sib)
@@ -98,15 +105,22 @@
     def gs_copy(step):
         return remote(g_send.at[step], g_recv.at[step], gs_s.at[step], gs_r.at[step], sib)
 
-    def rs_copy(step):
-        return remote(rs_send.at[step], rs_recv.at[step + 1], rs_s.at[step], rs_r.at[step + 1], nxt)
-
-    def rs_arrival(step):
-        return remote(rs_recv.at[step], rs_recv.at[step], rs_s.at[step], rs_r.at[step], nxt)
+    def rs_copy(step, piece):
+        return remote(
+            rs_send.at[step, piece], rs_recv.at[step + 1, piece],
+            rs_s.at[step, piece], rs_r.at[step + 1, piece], nxt,
+        )
+
+    def rs_arrival(step, piece):
+        return remote(
+            rs_recv.at[step, piece], rs_recv.at[step, piece],
+            rs_s.at[step, piece], rs_r.at[step, piece], nxt,
+        )
 
     pl.semaphore_wait(barrier, 3)
     local.wait()
-    ag_copy(0).start()
+    for piece in range(PIECES):
+        ag_copy(0, piece).start()
     sb_copy(0).start()
 
     @pl.loop(0, chips)
@@ -129,16 +143,17 @@
             w_col[k] = jnp.broadcast_to(weight * coef, (128, poles)).T
             acc[k] = jnp.zeros((rows, poles), jnp.float32)
 
-    def handle_gather(step):
-        ag_arrival(step).wait_recv()
+    def handle_gather(step, piece):
+        ag_arrival(step, piece).wait_recv()
 
         @pl.when(step < chips - 1)
         def _():
-            ag_copy(step).start()
-
-        sb_copy(step).start()
-
-    def compute(step):
+            ag_copy(step, piece).start()
+
+        if piece == PIECES - 1:
+            sb_copy(step).start()
+
+    def compute(step, between):
         sb_copy(step).wait_recv()
         meas_copy(0, step).wait()
         meas_copy(1, step).wait()
@@ -159,77 +174,92 @@
             gin_own = part if gin_own is None else gin_own + part
             part = stretched * jnp.dot(transposed, res_sib, preferred_element_type=jnp.float32)
             gin_sib = part if gin_sib is None else gin_sib + part
+            between(step, k)
         g_send[step] = gin_sib
         gs_copy(step).start()
         g_own[step] = gin_own
 
-    def encode(step, value):
+    def encode(step, piece, value):
         largest = jnp.maximum(jnp.max(jnp.abs(value), axis=0, keepdims=True), 1e-30)
         exponent = jnp.ceil(jnp.log2(largest) + 0.01) - 15.0
         coded = jnp.round(value * jnp.exp2(-exponent))
-        rs_send[step, :poles, :] = coded.astype(jnp.int32).astype(jnp.int16)
+        rs_send[step, piece, :share, :] = coded.astype(jnp.int32).astype(jnp.int16)
         tail = jnp.broadcast_to(exponent.astype(jnp.int32), (CODE, cols))
-        rs_send[step, poles:, :] = tail.astype(jnp.int16)
-
-    def decode(step):
-        tail = rs_recv[step, poles:, :].astype(jnp.int32).astype(jnp.float32)
-        return rs_recv[step, :poles, :].astype(jnp.int32).astype(jnp.float32) * jnp.exp2(tail[0:1])
-
-    def handle_sum(step):
-        gs_copy(step).wait_recv()
+        rs_send[step, piece, share:, :] = tail.astype(jnp.int16)
+
+    def decode(step, piece):
+        tail = rs_recv[step, piece, share:, :].astype(jnp.int32).astype(jnp.float32)
+        body = rs_recv[step, piece, :share, :].astype(jnp.int32).astype(jnp.float32)
+        return body * jnp.exp2(tail[0:1])
+
+    def chip_sum(step, piece):
+        part = pl.ds(piece * share, share)
+        return g_own[step, part, :] + g_recv[step, part, :]
+
+    def handle_sum(step, piece):
+        if piece == 0:
+            gs_copy(step).wait_recv()
 
         @pl.when(step == 1)
         def _():
-            encode(step, g_own[step] + g_recv[step])
+            encode(step, piece, chip_sum(step, piece))
 
         @pl.when(step > 1)
         def _():
-            rs_arrival(step).wait_recv()
-            encode(step, g_own[step] + g_recv[step] + decode(step))
+            rs_arrival(step, piece).wait_recv()
+            encode(step, piece, chip_sum(step, piece) + decode(step, piece))
 
         @pl.when(step > 0)
         def _():
-            rs_copy(step).start()
+            rs_copy(step, piece).start()
+
+    slots = 2 * PIECES
+
+    def between(step, k):
+        for slot in range(k * slots // combos, (k + 1) * slots // combos):
+            piece = slot % PIECES
+            if slot < PIECES:
+
+                @pl.when(step < chips - 1)
+                def _():
+                    handle_gather(step + 1, piece)
+            else:
+
+                @pl.when(step > 0)
+                def _():
+                    handle_sum(step - 1, piece)
 
     @pl.loop(0, chips)
     def _(step):
-        @pl.when((step > 0) & (step < chips - 1))
-        def _():
-            handle_gather(step + 1)
-
-        compute(step)
-
-        @pl.when(step == 0)
-        def _():
-            handle_gather(step + 1)
-
-        @pl.when(step > 0)
-        def _():
-            handle_sum(step - 1)
-
-    handle_sum(chips - 1)
+        compute(step, between)
+
+    for piece in range(PIECES):
+        handle_sum(chips - 1, piece)
 
     total = jnp.zeros((rows, poles), jnp.float32)
     for k in range(combos):
         total = total + w_row[k][0:1, :] * acc[k]
     grad_out[...] = total
 
-    rs_arrival(chips).wait_recv()
-    summed = g_own[0] + g_recv[0] + decode(chips)
-    grad_in[...] = summed.T
+    for piece in range(PIECES):
+        rs_arrival(chips, piece).wait_recv()
+        summed = chip_sum(0, piece) + decode(chips, piece)
+        grad_in[:, piece * share : (piece + 1) * share] = summed.T
 
     @pl.loop(0, chips)
     def _(step):
         sb_copy(step).wait_send()
         gs_copy(step).wait_send()
 
-        @pl.when(step < chips - 1)
-        def _():
-            ag_copy(step).wait_send()
-
-        @pl.when(step > 0)
-        def _():
-            rs_copy(step).wait_send()
+        for piece in range(PIECES):
+
+            @pl.when(step < chips - 1)
+            def _():
+                ag_copy(step, piece).wait_send()
+
+            @pl.when(step > 0)
+            def _():
+                rs_copy(step, piece).wait_send()
 
 
 def fused(measured, out_factor, in_factor, pole_rates, freq_index, quad_codes):
@@ -264,18 +294,18 @@
             pltpu.VMEM((chips, poles, cols), jnp.float32),
             pltpu.VMEM((chips, poles, cols), jnp.float32),
             pltpu.VMEM((chips, poles, cols), jnp.float32),
-            pltpu.VMEM((chips, poles + CODE, cols), jnp.int16),
-            pltpu.VMEM((chips + 1, poles + CODE, cols), jnp.int16),
+            pltpu.VMEM((chips, PIECES, poles // PIECES + CODE, cols), jnp.int16),
+            pltpu.VMEM((chips + 1, PIECES, poles // PIECES + CODE, cols), jnp.int16),
             dma,
             dma((2, chips)),
-            dma((chips,)),
-            dma((chips + 1,)),
+            dma((chips, PIECES)),
+            dma((chips + 1, PIECES)),
             dma((chips,)),
             dma((chips,)),
             dma((chips,)),
             dma((chips,)),
-            dma((chips + 1,)),
-            dma((chips + 1,)),
+            dma((chips + 1, PIECES)),
+            dma((chips + 1, PIECES)),
         ],
         compiler_params=pltpu.CompilerParams(
             collective_id=0, has_side_effects=True, vmem_limit_bytes=60 * 1024 * 1024

time: 68.4 us -> 60.2 us (0.88)
  Pallas kernels: 65.3 us -> 57.1 us
    pallas_call x1, Pallas kernels: 65.3 us -> 57.1 us  [fused(): call(measured.reshape(combos, rows, total_in), out_factor, in_factor, pol...]
where the time goes in v3:
time: 60.2 us; the launch traced here: 60 us
  Pallas kernels  57.1 us (95%)
  other arithmetic  2.26 us (4%)
  between operations  0.64 us (1%)
    pallas_call x1, Pallas kernels, fused(): call(measured.reshape(combos, rows, total_in), out_factor, in_factor, pol...  57.1 us
    mul x1, other arithmetic, fused(): grad_in * (1.0 / math.sqrt(total_out))  2.26 us

profile of v3, /device:TPU:0, one launch (start us, length us, event | category | flops | bytes accessed | tf_op | source)
XLA Modules:
  0.0 60.0 jit_solution(12007601214957859769)
XLA Ops:
  0.6 57.1 %shard_map.77 = (f32[256,512]{1,0:T(8,128)}, f32[256,512]{1,0:T(8,128)}) custom-call(bf16[4,256,4096]{2,1,0:T(8,128)(2,1)} %bitcast.2, bf16[256,512]{1,0:T(8,128)(2,1)} %out_factor.1, bf16[512,256]{1,0:T(8,128)(2,1)} %in_factor.1, f32[1,512]{1,0:T(1,128)} %bitcast.3, s32[2]{0:T(128)} %freq.1, s32[2]{0:T(128)} %quad.1), custom_call_target="tpu_custom_call" | custom-call | tf_op jit(solution)/shard_map/pallas_call | solution.py:314
  57.7 2.3 %broadcast_multiply_fusion = (f32[256,512]{1,0:T(8,128)}, f32[256,512]{1,0:T(8,128)}) fusion(f32[256,512]{1,0:T(8,128)} %get-tuple-element.5, f32[256,512]{1,0:T(8,128)} %get-tuple-element.4), kind=kLoop, calls=%fused_computation | loop fusion | flops 262144 | bytes 2097152 | tf_op jit(solution)/shard_map/mul | solution.py:322

commit v4 on v3

--- a/solution.py
+++ b/solution.py
@@ -175,7 +175,12 @@
             part = stretched * jnp.dot(transposed, res_sib, preferred_element_type=jnp.float32)
             gin_sib = part if gin_sib is None else gin_sib + part
             between(step, k)
-        g_send[step] = gin_sib
+        peak = jnp.maximum(jnp.max(jnp.abs(gin_sib), axis=0, keepdims=True), 1e-30)
+        power = jnp.ceil(jnp.log2(peak) + 0.01) - 15.0
+        coded = jnp.round(gin_sib * jnp.exp2(-power))
+        g_send[step, :poles, :] = coded.astype(jnp.int32).astype(jnp.int16)
+        ends = jnp.broadcast_to(power.astype(jnp.int32), (CODE, cols))
+        g_send[step, poles:, :] = ends.astype(jnp.int16)
         gs_copy(step).start()
         g_own[step] = gin_own
 
@@ -194,7 +199,9 @@
 
     def chip_sum(step, piece):
         part = pl.ds(piece * share, share)
-        return g_own[step, part, :] + g_recv[step, part, :]
+        ends = g_recv[step, poles:, :].astype(jnp.int32).astype(jnp.float32)
+        body = g_recv[step, part, :].astype(jnp.int32).astype(jnp.float32)
+        return g_own[step, part, :] + body * jnp.exp2(ends[0:1])
 
     def handle_sum(step, piece):
         if piece == 0:
@@ -292,8 +299,8 @@
             pltpu.VMEM((combos, poles, 128), jnp.float32),
             pltpu.VMEM((combos, rows, poles), jnp.float32),
             pltpu.VMEM((chips, poles, cols), jnp.float32),
-            pltpu.VMEM((chips, poles, cols), jnp.float32),
-            pltpu.VMEM((chips, poles, cols), jnp.float32),
+            pltpu.VMEM((chips, poles + CODE, cols), jnp.int16),
+            pltpu.VMEM((chips, poles + CODE, cols), jnp.int16),
             pltpu.VMEM((chips, PIECES, poles // PIECES + CODE, cols), jnp.int16),
             pltpu.VMEM((chips + 1, PIECES, poles // PIECES + CODE, cols), jnp.int16),
             dma,

time: 60.2 us -> 60.4 us (level)
  no operation moved by 1% of the time
where the time goes in v4:
time: 60.4 us; the launch traced here: 60.2 us
  Pallas kernels  57.3 us (95%)
  other arithmetic  2.26 us (4%)
  between operations  0.64 us (1%)
    pallas_call x1, Pallas kernels, fused(): call(measured.reshape(combos, rows, total_in), out_factor, in_factor, pol...  57.3 us
    mul x1, other arithmetic, fused(): grad_in * (1.0 / math.sqrt(total_out))  2.26 us

profile of v4, /device:TPU:0, one launch (start us, length us, event | category | flops | bytes accessed | tf_op | source)
XLA Modules:
  0.0 60.2 jit_solution(9897207196035446192)
XLA Ops:
  0.6 57.3 %shard_map.77 = (f32[256,512]{1,0:T(8,128)}, f32[256,512]{1,0:T(8,128)}) custom-call(bf16[4,256,4096]{2,1,0:T(8,128)(2,1)} %bitcast.2, bf16[256,512]{1,0:T(8,128)(2,1)} %out_factor.1, bf16[512,256]{1,0:T(8,128)(2,1)} %in_factor.1, f32[1,512]{1,0:T(1,128)} %bitcast.3, s32[2]{0:T(128)} %freq.1, s32[2]{0:T(128)} %quad.1), custom_call_target="tpu_custom_call" | custom-call | tf_op jit(solution)/shard_map/pallas_call | solution.py:321
  58.0 2.3 %broadcast_multiply_fusion = (f32[256,512]{1,0:T(8,128)}, f32[256,512]{1,0:T(8,128)}) fusion(f32[256,512]{1,0:T(8,128)} %get-tuple-element.5, f32[256,512]{1,0:T(8,128)} %get-tuple-element.4), kind=kLoop, calls=%fused_computation | loop fusion | flops 262144 | bytes 2097152 | tf_op jit(solution)/shard_map/mul | solution.py:329
